TPU v7x, 32 devices: a whole 2x2x4 slice. The times are simulated.
32 devices in a mesh: dp: 8 (over z, y), tensor: 4 (over x, core).
Axes of the slice: x: 2, y: 2, z: 4, core: 2. Of those that a mesh axis runs over, the one named last changes fastest.
Arguments:
- tokens: bfloat16 [16384, 768], P(('dp', 'tensor')), may hold values from -6 to 6
- gene_counts: int32 [16], P('dp'), may hold values from 300 to 1024, as said below
- in_proj: bfloat16 [3, 768, 768], P(None, None, 'tensor'), may hold values from -0.21875 to 0.21875
- out_proj: bfloat16 [768, 768], P('tensor'), may hold values from -0.875 to 0.875
- up_proj: bfloat16 [768, 3072], P(None, 'tensor'), may hold values from -0.21875 to 0.21875
- down_proj: bfloat16 [3072, 768], P('tensor'), may hold values from -0.109375 to 0.109375
- gains: float32 [2, 768], replicated, may hold values from 0.1 to 1.9
- biases: float32 [2, 768], replicated, may hold values from -3 to 3
- cotangent: bfloat16 [16384, 768], P(('dp', 'tensor')), may hold values from -6 to 6
Outputs:
- block_out: bfloat16 [16384, 768], P(('dp', 'tensor'))
- input_grad: bfloat16 [16384, 768], P(('dp', 'tensor'))
- grad_in_proj: float32 [3, 768, 768], P(None, 'dp', 'tensor')
- grad_out_proj: float32 [768, 768], P('tensor', 'dp')
- grad_up_proj: float32 [768, 3072], P('dp', 'tensor')
- grad_down_proj: float32 [3072, 768], P('tensor', 'dp')
- grad_gains: float32 [2, 768], replicated
- grad_biases: float32 [2, 768], replicated
Inputs may be any that keep to these rules, and one draw needn't show every extreme that they name: Cell c holds genes at its first gene_counts[c] positions and padding at the rest of its 1024 positions; in every draw one cell holds 1024 genes and one holds 300; most cells are short.
All inputs are finite; a program needn't handle non-finite values.
Results may differ from a plain program's by a relative error of at most 0.013.
The roundings to bfloat16 on the way count: a program that leaves them out, or rounds other values in their place, can miss the bound.
Values may be sent and summed in bfloat16 or wider, within the bound.
A program may use at most 128 MiB of HBM per device.

v0:
```python
import jax
import jax.numpy as jnp
from jax import lax
from jax.sharding import PartitionSpec as P

HEAD_DIM = 64
EPS = 1e-05
NEG = -1e30


def layer_norm(values, gain, offset):
    center = values - jnp.mean(values, axis=-1, keepdims=True)
    spread = jnp.mean(center * center, axis=-1, keepdims=True)
    return center * lax.rsqrt(spread + EPS) * gain + offset


def gelu_exact(values):
    return jax.nn.gelu(values, approximate=False)


def per_device(
    tokens, gene_counts, in_proj, out_proj, up_proj, down_proj, gains, biases, cotangent
):
    rows = tokens.shape[0]
    cells = gene_counts.shape[0]
    group = rows * lax.axis_size("tensor")
    length = group // cells
    local_width = out_proj.shape[0]
    heads = local_width // HEAD_DIM
    block = min(length, 512)
    blocks = length // block
    scale = HEAD_DIM ** (-0.5)
    positions = jnp.arange(length, dtype=jnp.int32)
    resid = tokens.astype(jnp.float32)
    normed, first_back = jax.vjp(layer_norm, resid, gains[0], biases[0])
    normed_all = lax.all_gather(normed.astype(jnp.bfloat16), "tensor", axis=0, tiled=True)
    projected = jnp.einsum(
        "td,cde->cte", normed_all, in_proj, preferred_element_type=jnp.float32
    ).astype(jnp.bfloat16)
    query_cells = projected[0].reshape(cells, blocks, block, local_width)
    key_cells = projected[1].reshape(cells, length, local_width)
    value_cells = projected[2].reshape(cells, length, local_width)

    def block_scores(query_block, key_rows, count):
        query_heads = query_block.reshape(block, heads, HEAD_DIM)
        key_heads = key_rows.reshape(length, heads, HEAD_DIM)
        scores = (
            jnp.einsum("qhd,khd->hqk", query_heads, key_heads, preferred_element_type=jnp.float32)
            * scale
        )
        return jnp.where((positions < count)[None, None, :], scores, NEG)

    def cell_forward(item):
        queries, key_rows, value_rows, count = item
        value_heads = value_rows.reshape(length, heads, HEAD_DIM)

        def one_block(query_block):
            scores = block_scores(query_block, key_rows, count)
            top = jnp.max(scores, axis=-1, keepdims=True)
            expo = jnp.exp(scores - top)
            total = jnp.sum(expo, axis=-1, keepdims=True)
            probs = (expo / total).astype(jnp.bfloat16)
            result = jnp.einsum(
                "hqk,khd->qhd", probs, value_heads, preferred_element_type=jnp.float32
            )
            return (
                result.reshape(block, local_width).astype(jnp.bfloat16),
                (top + jnp.log(total))[..., 0],
            )

        return lax.map(one_block, queries)

    attended, log_totals = lax.map(cell_forward, (query_cells, key_cells, value_cells, gene_counts))
    attended = attended.reshape(group, local_width)
    piece = attended
    mid = resid + lax.psum_scatter(
        jnp.dot(piece, out_proj, preferred_element_type=jnp.float32),
        "tensor",
        scatter_dimension=0,
        tiled=True,
    )
    normed_mid, second_back = jax.vjp(layer_norm, mid, gains[1], biases[1])
    mid_low = normed_mid.astype(jnp.bfloat16)
    mid_all = lax.all_gather(mid_low, "tensor", axis=0, tiled=True)
    hidden = jnp.dot(mid_all, up_proj, preferred_element_type=jnp.float32)
    active = gelu_exact(hidden).astype(jnp.bfloat16)
    piece = active
    block_out = (
        mid
        + lax.psum_scatter(
            jnp.dot(piece, down_proj, preferred_element_type=jnp.float32).astype(jnp.bfloat16),
            "tensor",
            scatter_dimension=0,
            tiled=True,
        ).astype(jnp.float32)
    ).astype(jnp.bfloat16)
    out_grads = lax.all_gather(cotangent, "tensor", axis=0, tiled=True)
    _, gelu_back = jax.vjp(gelu_exact, hidden)
    active_grad = jnp.einsum("td,fd->tf", out_grads, down_proj, preferred_element_type=jnp.float32)
    hidden_grad = gelu_back(active_grad)[0].astype(jnp.bfloat16)
    grad_down = jnp.einsum("tf,td->fd", active, out_grads, preferred_element_type=jnp.float32)
    grad_up = jnp.einsum("td,tf->df", mid_all, hidden_grad, preferred_element_type=jnp.float32)
    piece = hidden_grad
    mid_grad = lax.psum_scatter(
        jnp.einsum("tf,df->td", piece, up_proj, preferred_element_type=jnp.float32),
        "tensor",
        scatter_dimension=0,
        tiled=True,
    )
    resid_part, gain_second, bias_second = second_back(mid_grad)
    mid_total = cotangent.astype(jnp.float32) + resid_part
    branch_all = lax.all_gather(mid_total.astype(jnp.bfloat16), "tensor", axis=0, tiled=True)
    attended_grad = jnp.einsum(
        "td,ed->te", branch_all, out_proj, preferred_element_type=jnp.float32
    ).astype(jnp.bfloat16)
    grad_out = jnp.einsum("te,td->ed", attended, branch_all, preferred_element_type=jnp.float32)

    def cell_backward(item):
        queries, key_rows, value_rows, count, grad_rows, totals = item
        key_heads = key_rows.reshape(length, heads, HEAD_DIM)
        value_heads = value_rows.reshape(length, heads, HEAD_DIM)

        def one_block(carry, part):
            key_sum, value_sum = carry
            query_block, grad_block, total_block = part
            scores = block_scores(query_block, key_rows, count)
            probs = jnp.exp(scores - total_block[..., None])
            grad_heads = grad_block.reshape(block, heads, HEAD_DIM)
            query_heads = query_block.reshape(block, heads, HEAD_DIM)
            prob_grads = jnp.einsum(
                "qhd,khd->hqk", grad_heads, value_heads, preferred_element_type=jnp.float32
            )
            inner = jnp.sum(probs * prob_grads, axis=-1, keepdims=True)
            score_grads = (probs * (prob_grads - inner)).astype(jnp.bfloat16)
            query_grad = (
                jnp.einsum(
                    "hqk,khd->qhd", score_grads, key_heads, preferred_element_type=jnp.float32
                )
                * scale
            )
            key_sum = (
                key_sum
                + jnp.einsum(
                    "hqk,qhd->khd", score_grads, query_heads, preferred_element_type=jnp.float32
                )
                * scale
            )
            value_sum = value_sum + jnp.einsum(
                "hqk,qhd->khd",
                probs.astype(jnp.bfloat16),
                grad_heads,
                preferred_element_type=jnp.float32,
            )
            return (
                (key_sum, value_sum),
                query_grad.reshape(block, local_width).astype(jnp.bfloat16),
            )

        zeros = jnp.zeros((length, heads, HEAD_DIM), jnp.float32)
        (key_sum, value_sum), query_grads = lax.scan(
            one_block, (zeros, zeros), (queries, grad_rows, totals)
        )
        return (
            query_grads.reshape(length, local_width),
            key_sum.reshape(length, local_width).astype(jnp.bfloat16),
            value_sum.reshape(length, local_width).astype(jnp.bfloat16),
        )

    grad_cells = attended_grad.reshape(cells, blocks, block, local_width)
    query_grads, key_grads, value_grads = lax.map(
        cell_backward, (query_cells, key_cells, value_cells, gene_counts, grad_cells, log_totals)
    )
    proj_grads = jnp.stack(
        [
            query_grads.reshape(group, local_width),
            key_grads.reshape(group, local_width),
            value_grads.reshape(group, local_width),
        ]
    )
    grad_in = jnp.einsum("td,cte->cde", normed_all, proj_grads, preferred_element_type=jnp.float32)
    piece = proj_grads
    normed_grad = lax.psum_scatter(
        jnp.einsum("cte,cde->td", piece, in_proj, preferred_element_type=jnp.float32),
        "tensor",
        scatter_dimension=0,
        tiled=True,
    )
    resid_grad, gain_first, bias_first = first_back(normed_grad)
    input_grad = (mid_total + resid_grad).astype(jnp.bfloat16)
    grad_gains, grad_biases = lax.psum(
        (jnp.stack([gain_first, gain_second]), jnp.stack([bias_first, bias_second])),
        ("dp", "tensor"),
    )
    grad_in_part, grad_out_part, grad_up_part, grad_down_part = (
        lax.psum_scatter(grad_in, "dp", scatter_dimension=1, tiled=True),
        lax.psum_scatter(grad_out, "dp", scatter_dimension=1, tiled=True),
        lax.psum_scatter(grad_up, "dp", scatter_dimension=0, tiled=True),
        lax.psum_scatter(grad_down, "dp", scatter_dimension=1, tiled=True),
    )
    return (
        block_out,
        input_grad,
        grad_in_part,
        grad_out_part,
        grad_up_part,
        grad_down_part,
        grad_gains,
        grad_biases,
    )


def solution(mesh):
    placed = (
        P(("dp", "tensor"), None),
        P("dp"),
        P(None, None, "tensor"),
        P("tensor", None),
        P(None, "tensor"),
        P("tensor", None),
        P(),
        P(),
        P(("dp", "tensor"), None),
    )
    return jax.shard_map(
        per_device,
        mesh=mesh,
        in_specs=placed,
        out_specs=(
            P(("dp", "tensor"), None),
            P(("dp", "tensor"), None),
            P(None, "dp", "tensor"),
            P("tensor", "dp"),
            P("dp", "tensor"),
            P("tensor", "dp"),
            P(),
            P(),
        ),
        check_vma=False,
    )
```

profile of v0, /device:TPU:0, one launch (start us, length us, event | category | flops | bytes accessed | tf_op | source)
XLA Modules:
  0.0 751.3 jit_solution(6833605343567260367)
XLA Ops:
  14.6 31.3 %all-gather.5.cloned.1.call-done = bf16[2048,768]{1,0:T(8,128)(2,1)} async-done(((bf16[512,768]{1,0:T(8,128)(2,1)}), bf16[2048,768]{1,0:T(8,128)(2,1)}) %all-gather.5.cloned.1.call-update) | async-done | bytes 3145744 | tf_op jit(solution)/shard_map/all_gather | solution.py:36
  45.9 3.9 fusion.59
  55.7 40.2 %while.58 = (s32[]{:T(128)}, bf16[2,2,512,192]{2,1,0,3:T(2,128)(2,1)}, f32[2,2,3,512]{3,2,1,0:T(4,128)}, bf16[2,2,512,192]{2,3,1,0:T(8,128)(2,1)S(1)}, bf16[2,10...) while((s32[]{:T(128)}, ...), condition=%wide.region_7.8_spmd.clone, body=%wide.region_2.7_spmd.clone.sunk | while | flops 421625344 | bytes 28903900 | solution.py:73
  58.8 13.5 %while.61 = (s32[]{:T(128)}, bf16[2,512,192]{1,2,0:T(8,128)(2,1)}, f32[2,3,512]{2,1,0:T(4,128)}, s32[]{:T(128)}, s32[1024]{0:T(1024)S(1)}, /*index=5*/bf16[2,512...) while((s32[]{:T(128)}, bf16[2,512,192]{1,2,0:T(8,128)(2,1)}, ...), condition=%wide.region_6.6_spmd, body=%wide.region_3.5_spmd.sunk | while | flops 421625344 | bytes 25721088 | solution.py:71
  78.9 13.5 %while.61 = (s32[]{:T(128)}, bf16[2,512,192]{1,2,0:T(8,128)(2,1)}, f32[2,3,512]{2,1,0:T(4,128)}, s32[]{:T(128)}, s32[1024]{0:T(1024)S(1)}, /*index=5*/bf16[2,512...) while((s32[]{:T(128)}, bf16[2,512,192]{1,2,0:T(8,128)(2,1)}, ...), condition=%wide.region_6.6_spmd, body=%wide.region_3.5_spmd.sunk | while | flops 421625344 | bytes 25721088 | solution.py:71
  98.7 4.9 fusion.60
  103.8 58.3 %reduce-scatter.13.cloned.1.call-done = f32[512,768]{1,0:T(8,128)} async-done(((f32[2048,768]{1,0:T(8,128)}), f32[512,768]{1,0:T(8,128)}) %reduce-scatter.13.cloned.1.call-update) | async-done | bytes 1572880 | tf_op jit(solution)/shard_map/reduce_scatter | solution.py:76
  166.8 28.1 %all-gather.7.cloned.1.call-done = bf16[2048,768]{1,0:T(8,128)(2,1)} async-done(((bf16[512,768]{1,0:T(8,128)(2,1)}), bf16[2048,768]{1,0:T(8,128)(2,1)}) %all-gather.7.cloned.1.call-update) | async-done | bytes 3145744 | tf_op jit(solution)/shard_map/all_gather | solution.py:84
  194.9 7.5 fusion.61
  202.3 22.6 %all-gather.9.cloned.1.call-done = bf16[2048,768]{1,0:T(8,128)(2,1)} async-done(((bf16[512,768]{1,0:T(8,128)(2,1)}), bf16[2048,768]{1,0:T(8,128)(2,1)}) %all-gather.9.cloned.1.call-update) | async-done | bytes 3145744 | tf_op jit(solution)/shard_map/all_gather | solution.py:97
  224.9 19.2 %add_convert_fusion = (bf16[2048,768]{1,0:T(8,128)(2,1)S(1)}, f32[2048,768]{1,0:T(8,128)}) fusion(f32[2048,768]{1,0:T(8,128)} %fusion.61, bf16[2048,768]{1,0:T(8,128)(2,1)} %all-gather.9.cloned.1.call-done, bf16[768,768]{1,0:T(8,128)(2,1)S(1)} %copy-done), kind=kOutput, calls=%fused_computation.51 | convolution fusion | flops 2529165312 | bytes 20054016 | tf_op jit(solution)/shard_map/td,fd->tf/dot_general | solution.py:99
  245.8 4.5 fusion.62
  250.4 5.5 multiply_convert_fusion.1
  257.6 4.0 convolution_convert_fusion
  261.9 47.0 %reduce-scatter.17.cloned.1.call-done = f32[512,768]{1,0:T(8,128)} async-done(((f32[2048,768]{1,0:T(8,128)}), f32[512,768]{1,0:T(8,128)}) %reduce-scatter.17.cloned.1.call-update) | async-done | bytes 1572880 | tf_op jit(solution)/shard_map/reduce_scatter | solution.py:104
  311.5 37.8 %reduce-scatter.15.cloned.1.call-done = bf16[512,768]{1,0:T(8,128)(2,1)} async-done(((bf16[2048,768]{1,0:T(8,128)(2,1)}), bf16[512,768]{1,0:T(8,128)(2,1)}) %reduce-scatter.15.cloned.1.call-update) | async-done | bytes 786448 | tf_op jit(solution)/shard_map/reduce_scatter | solution.py:90
  354.9 28.6 %all-gather.11.cloned.1.call-done = bf16[2048,768]{1,0:T(8,128)(2,1)} async-done(((bf16[512,768]{1,0:T(8,128)(2,1)}), bf16[2048,768]{1,0:T(8,128)(2,1)}) %all-gather.11.cloned.1.call-update) | async-done | bytes 3145744 | tf_op jit(solution)/shard_map/all_gather | solution.py:112
  387.1 4.1 convolution_bitcast_fusion.1
  391.3 62.7 %while.60 = (s32[]{:T(128)}, bf16[2,1024,192]{2,1,0:T(8,128)(2,1)}, bf16[2,1024,192]{1,2,0:T(8,128)(2,1)}, bf16[2,1024,192]{1,2,0:T(8,128)(2,1)}, bf16[2,2,512,1...) while((s32[]{:T(128)}, bf16[2,1024,192]{2,1,0:T(8,128)(2,1)}, ...), condition=%wide.region_19.20_spmd.clone, body=%wide.region_15.19_spmd.clone.sunk | while | flops 1031798272 | bytes 92420848 | solution.py:170
  396.5 21.5 %while.62 = (s32[]{:T(128)}, f32[1024,3,64]{0,2,1:T(8,128)S(1)}, f32[1024,3,64]{0,2,1:T(8,128)}, bf16[2,512,192]{1,2,0:T(8,128)(2,1)}, bf16[2,512,192]{1,2,0:T(8...) while((s32[]{:T(128)}, f32[1024,3,64]{0,2,1:T(8,128)S(1)}, ...), condition=%wide.region_18.18_spmd.clone, body=%wide.region_16.17_spmd.clone.sunk | while | flops 1031405056 | bytes 63162644 | solution.py:160
  427.8 21.5 %while.62 = (s32[]{:T(128)}, f32[1024,3,64]{0,2,1:T(8,128)S(1)}, f32[1024,3,64]{0,2,1:T(8,128)}, bf16[2,512,192]{1,2,0:T(8,128)(2,1)}, bf16[2,512,192]{1,2,0:T(8...) while((s32[]{:T(128)}, f32[1024,3,64]{0,2,1:T(8,128)S(1)}, ...), condition=%wide.region_18.18_spmd.clone, body=%wide.region_16.17_spmd.clone.sunk | while | flops 1031405056 | bytes 63162644 | solution.py:160
  459.9 4.1 fusion.44
  466.8 4.8 reshape.219
  471.7 4.6 convolution_bitcast_fusion
  476.3 7.0 fusion.64
  483.6 7.0 fusion.63
  493.5 45.0 %reduce-scatter.25.cloned.1.call-done = f32[96,576]{1,0:T(8,128)} async-done(((f32[768,576]{1,0:T(8,128)}), f32[96,576]{1,0:T(8,128)}) %reduce-scatter.25.cloned.1.call-update) | async-done | bytes 221200
  540.4 58.0 %reduce-scatter.19.cloned.1.call-done = f32[512,768]{1,0:T(8,128)} async-done(((f32[2048,768]{1,0:T(8,128)}), f32[512,768]{1,0:T(8,128)}) %reduce-scatter.19.cloned.1.call-update) | async-done | bytes 1572880 | tf_op jit(solution)/shard_map/reduce_scatter | solution.py:182
  604.4 40.3 %all-reduce = (f32[2,768]{1,0:T(2,128)}, f32[2,768]{1,0:T(2,128)}) all-reduce(f32[2,768]{1,0:T(2,128)} %pad_maximum_fusion.3, f32[2,768]{1,0:T(2,128)} %pad_maximum_fusion.4), channel_id=1, replica_groups=mesh['dp'=8,'tensor'=4] {'dp','tensor'}, use_global_device_ids=true, to_apply=%region_29.30 | all-reduce | flops 3072 | bytes 24576 | tf_op jit(solution)/shard_map/psum | solution.py:190
  645.4 3.2 add_convert_fusion.1
  648.6 23.5 %reduce-scatter.23.cloned.1.call-done = f32[768,96]{0,1:T(8,128)} async-done(((f32[768,768]{0,1:T(8,128)}), f32[768,96]{0,1:T(8,128)}) %reduce-scatter.23.cloned.1.call-update) | async-done | bytes 294928 | tf_op jit(solution)/shard_map/reduce_scatter | solution.py:198
  672.1 72.2 %reduce-scatter.21.cloned.1.call-done = f32[96,768]{1,0:T(8,128)} async-done(((f32[768,768]{1,0:T(8,128)}), f32[96,768]{1,0:T(8,128)}) %reduce-scatter.21.cloned.1.call-update) | async-done | bytes 294928 | tf_op jit(solution)/shard_map/reduce_scatter | solution.py:197
  (352 shorter events, 158.6 us)
Async XLA Ops:
  7.2 217.7 %copy-start = (bf16[768,768]{1,0:T(8,128)(2,1)S(1)}, bf16[768,768]{1,0:T(8,128)(2,1)}, u32[]{:S(2)}) copy-start(bf16[768,768]{1,0:T(8,128)(2,1)} %param.22) | copy-start | bytes 3538948
  7.2 38.8 %copy-start.42 = (bf16[3,768,192]{1,2,0:T(8,128)(2,1)S(1)}, bf16[3,768,192]{1,2,0:T(8,128)(2,1)}, u32[]{:S(2)}) copy-start(bf16[3,768,192]{1,2,0:T(8,128)(2,1)} %param.19) | copy-start | bytes 2654212
  7.2 38.7 %all-gather.5.cloned.1.call-start = ((), (), s32[]{:S(2)}) async-start(), calls=%async_computation.8 | async-start | bytes 3932160 | tf_op jit(solution)/shard_map/all_gather | solution.py:36
  8.7 41.2 %copy-start.31 = (f32[512]{0:T(512)}, f32[512]{0:T(512)S(1)}, u32[]{:S(2)}) copy-start(f32[512]{0:T(512)S(1)} %broadcast_multiply_fusion.1) | copy-start | bytes 6148
  10.8 39.1 %copy-start.34 = (f32[512]{0:T(512)}, f32[512]{0:T(512)S(1)}, u32[]{:S(2)}) copy-start(f32[512]{0:T(512)S(1)} %fusion.48) | copy-start | bytes 6148
  12.2 37.7 %copy-start.29 = (f32[768]{0:T(1024)}, f32[768]{0:T(1024)S(1)}, u32[]{:S(2)}) copy-start(f32[768]{0:T(1024)S(1)} %get-tuple-element.496) | copy-start | bytes 9220
  14.6 147.5 %reduce-scatter.13.cloned.1.call-start = ((), (), s32[]{:S(2)}) async-start(), calls=%async_computation.9 | async-start | bytes 7864320 | tf_op jit(solution)/shard_map/reduce_scatter | solution.py:76
  95.9 7.7 %copy-start.3 = (bf16[2,2,512,192]{2,3,1,0:T(8,128)(2,1)}, bf16[2,2,512,192]{2,3,1,0:T(8,128)(2,1)S(1)}, u32[]{:S(2)}) copy-start(bf16[2,2,512,192]{2,3,1,0:T(8,128)(2,1)S(1)} %get-tuple-element.948) | copy-start | bytes 2359300
  103.6 60.7 %copy-start.33 = (f32[768]{0:T(1024)S(1)}, f32[768]{0:T(1024)}, u32[]{:S(2)}) copy-start(f32[768]{0:T(1024)} %get-tuple-element.497) | copy-start | bytes 9220
  103.6 91.3 %all-gather.7.cloned.1.call-start = ((), (), s32[]{:S(2)}) async-start(), calls=%async_computation.10 | async-start | bytes 3932160 | tf_op jit(solution)/shard_map/all_gather | solution.py:84
  166.2 58.8 %all-gather.9.cloned.1.call-start = ((), (), s32[]{:S(2)}) async-start(), calls=%async_computation.12 | async-start | bytes 3932160 | tf_op jit(solution)/shard_map/all_gather | solution.py:97
  166.7 142.1 %reduce-scatter.17.cloned.1.call-start = ((), (), s32[]{:S(2)}) async-start(), calls=%async_computation.13 | async-start | bytes 7864320 | tf_op jit(solution)/shard_map/reduce_scatter | solution.py:104
  224.9 20.9 %copy-start.41 = (bf16[768,768]{1,0:T(8,128)(2,1)S(1)}, bf16[768,768]{1,0:T(8,128)(2,1)}, u32[]{:S(2)}) copy-start(bf16[768,768]{1,0:T(8,128)(2,1)} %param.21) | copy-start | bytes 3538948
  250.4 98.9 %reduce-scatter.15.cloned.1.call-start = ((), (), s32[]{:S(2)}) async-start(), calls=%async_computation.11 | async-start | bytes 3932160 | tf_op jit(solution)/shard_map/reduce_scatter | solution.py:90
  261.6 121.9 %all-gather.11.cloned.1.call-start = ((), (), s32[]{:S(2)}) async-start(), calls=%async_computation.14 | async-start | bytes 3932160 | tf_op jit(solution)/shard_map/all_gather | solution.py:112
  311.5 42.1 %copy-start.15 = (bf16[512,768]{1,0:T(8,128)(2,1)S(1)}, bf16[512,768]{1,0:T(8,128)(2,1)}, u32[]{:S(2)}) copy-start(bf16[512,768]{1,0:T(8,128)(2,1)} %param.25) | copy-start | bytes 2359300
  352.4 31.1 %copy-start.28 = (bf16[192,768]{1,0:T(8,128)(2,1)S(1)}, bf16[192,768]{1,0:T(8,128)(2,1)}, u32[]{:S(2)}) copy-start(bf16[192,768]{1,0:T(8,128)(2,1)} %param.20) | copy-start | bytes 884740
  352.4 34.1 %copy-start.38 = (f32[512]{0:T(512)}, f32[512]{0:T(512)S(1)}, u32[]{:S(2)}) copy-start(f32[512]{0:T(512)S(1)} %negate_multiply_fusion.2) | copy-start | bytes 6148
  354.8 137.1 %reduce-scatter.27.cloned.1.call-start = ((), (), s32[]{:S(2)}) async-start(), calls=%async_computation.19 | async-start | bytes 884736
  354.9 32.3 %copy-start.17 = (bf16[2048,192]{0,1:T(8,128)(2,1)S(1)}, bf16[2048,192]{0,1:T(8,128)(2,1)}, u32[]{:S(2)}) copy-start(bf16[2048,192]{0,1:T(8,128)(2,1)} %copy-done.16) | copy-start | bytes 2359300
  391.3 147.3 %reduce-scatter.25.cloned.1.call-start = ((), (), s32[]{:S(2)}) async-start(), calls=%async_computation.18 | async-start | bytes 2211840
  471.6 126.8 %reduce-scatter.19.cloned.1.call-start = ((), (), s32[]{:S(2)}) async-start(), calls=%async_computation.15 | async-start | bytes 7864320 | tf_op jit(solution)/shard_map/reduce_scatter | solution.py:182
  476.3 195.8 %reduce-scatter.23.cloned.1.call-start = ((), (), s32[]{:S(2)}) async-start(), calls=%async_computation.17 | async-start | bytes 2654208 | tf_op jit(solution)/shard_map/reduce_scatter | solution.py:198
  483.4 7.3 copy-start.40
  483.4 7.9 %copy-start.39 = (f32[768]{0:T(1024)S(1)}, f32[768]{0:T(1024)}, u32[]{:S(2)}) copy-start(f32[768]{0:T(1024)} %get-tuple-element.397) | copy-start | bytes 9220
  483.4 260.9 %reduce-scatter.21.cloned.1.call-start = ((), (), s32[]{:S(2)}) async-start(), calls=%async_computation.16 | async-start | bytes 2654208 | tf_op jit(solution)/shard_map/reduce_scatter | solution.py:197
  490.6 107.8 %copy-start.2 = (bf16[512,768]{1,0:T(8,128)(2,1)S(1)}, bf16[512,768]{1,0:T(8,128)(2,1)}, u32[]{:S(2)}) copy-start(bf16[512,768]{1,0:T(8,128)(2,1)} %param.17) | copy-start | bytes 2359300
  490.6 107.8 %copy-start.30 = (f32[768]{0:T(1024)S(1)}, f32[768]{0:T(1024)}, u32[]{:S(2)}) copy-start(f32[768]{0:T(1024)} %copy-done.29) | copy-start | bytes 9220
  490.7 107.8 %copy-start.32 = (f32[512]{0:T(512)S(1)}, f32[512]{0:T(512)}, u32[]{:S(2)}) copy-start(f32[512]{0:T(512)} %copy-done.31) | copy-start | bytes 6148
  490.7 109.8 %copy-start.37 = (f32[512]{0:T(512)S(1)}, f32[512]{0:T(512)}, u32[]{:S(2)}) copy-start(f32[512]{0:T(512)} %copy-done.36) | copy-start | bytes 6148
  490.7 109.8 %copy-start.35 = (f32[512]{0:T(512)S(1)}, f32[512]{0:T(512)}, u32[]{:S(2)}) copy-start(f32[512]{0:T(512)} %copy-done.34) | copy-start | bytes 6148
  600.5 143.8 %copy-start.1 = (bf16[768,768]{1,0:T(8,128)(2,1)S(1)}, bf16[768,768]{1,0:T(8,128)(2,1)}, u32[]{:S(2)}) copy-start(bf16[768,768]{1,0:T(8,128)(2,1)} %param.22) | copy-start | bytes 3538948
  (58 other events, 110.3 us)
Sparse Core Ops, SparseCore 0:
  14.7 31.2 all-gather.4
  103.7 58.3 reduce-scatter.12
  166.3 28.5 all-gather.6
  196.3 28.5 all-gather.8
  250.5 58.3 reduce-scatter.16
  311.3 37.9 reduce-scatter.14
  354.9 28.5 all-gather.10
  391.4 62.4 reduce-scatter.26
  471.7 66.7 reduce-scatter.24
  541.1 57.2 reduce-scatter.18
  602.5 69.5 reduce-scatter.22
  676.0 68.1 reduce-scatter.20
where the time goes:
time: 761 us; the launch traced here: 751 us
  waiting for transfers between devices  453 us (60%)
  matrix products  112 us (15%)
  local copies, waits for them, and re-layouts  73.3 us (10%)
  other arithmetic  55.6 us (7%)
  blocking collectives  40.3 us (5%)
  between operations  14.8 us (2%)
    reduce_scatter x1, waiting for transfers between devices, per_device(): lax.psum_scatter(grad_up, 'dp', scatter_dimension=0, tiled=True)  72.2 us
    reduce_scatter x1, waiting for transfers between devices, per_device(): lax.psum_scatter(jnp.dot(piece, out_proj, preferred_element_type=jnp.floa...  58.3 us
    reduce_scatter x1, waiting for transfers between devices, per_device(): lax.psum_scatter(jnp.einsum('cte,cde->td', piece, in_proj, preferred_elem...  58 us
    reduce_scatter x1, waiting for transfers between devices, per_device(): lax.psum_scatter(jnp.einsum('tf,df->td', piece, up_proj, preferred_elemen...  47 us
    unnamed x14, waiting for transfers between devices  45.7 us
    psum x1, blocking collectives, per_device(): lax.psum((jnp.stack([gain_first, gain_second]), jnp.stack([bias_first, bi...  40.3 us
    reduce_scatter x1, waiting for transfers between devices, per_device(): lax.psum_scatter(jnp.dot(piece, down_proj, preferred_element_type=jnp.flo...  37.8 us
    all_gather x1, waiting for transfers between devices, per_device(): lax.all_gather(normed.astype(jnp.bfloat16), 'tensor', axis=0, tiled=True)  31.3 us
  transfers between devices with their start and end apart: 12, of which 11 were waited for; matrix products, arithmetic and copies ran while one was open for 17% of the time, Pallas kernels for 0%

commit v1 on v0

--- a/solution.py
+++ b/solution.py
@@ -6,6 +6,25 @@
 HEAD_DIM = 64
 EPS = 1e-05
 NEG = -1e30
+
+
+def joined_along(tiles, dim):
+    tiles = jnp.moveaxis(tiles, 0, dim)
+    dims = tiles.shape
+    return tiles.reshape(*dims[:dim], dims[dim] * dims[dim + 1], *dims[dim + 2 :])
+
+
+def grow_blocks(array, axis):
+    length, position = (lax.axis_size(axis), lax.axis_index(axis))
+    tiles, bit = (array[None], 1)
+    while bit < length:
+        partner_block = lax.ppermute(tiles, axis, [(i, i ^ bit) for i in range(length)])
+        low = position & bit == 0
+        tiles = jnp.concatenate(
+            [jnp.where(low, tiles, partner_block), jnp.where(low, partner_block, tiles)]
+        )
+        bit *= 2
+    return tiles
 
 
 def layer_norm(values, gain, offset):
@@ -33,7 +52,8 @@
     positions = jnp.arange(length, dtype=jnp.int32)
     resid = tokens.astype(jnp.float32)
     normed, first_back = jax.vjp(layer_norm, resid, gains[0], biases[0])
-    normed_all = lax.all_gather(normed.astype(jnp.bfloat16), "tensor", axis=0, tiled=True)
+    x = normed.astype(jnp.bfloat16)
+    normed_all = joined_along(grow_blocks(x, "tensor"), 0)
     projected = jnp.einsum(
         "td,cde->cte", normed_all, in_proj, preferred_element_type=jnp.float32
     ).astype(jnp.bfloat16)

time: 761 us -> 768 us (level)
  waiting for transfers between devices: 453 us -> 461 us
    ppermute x0 -> x2, waiting for transfers between devices: none -> 37.1 us  [grow_blocks(): lax.ppermute(tiles, axis, [(i, i ^ bit) for i in range(length)])]
    all_gather x1 -> x0, waiting for transfers between devices: 31.3 us -> none  [per_device(): lax.all_gather(normed.astype(jnp.bfloat16), 'tensor', axis=0, tiled=True)]
    unnamed x68 -> x78, local copies, waits for them, and re-layouts: 18.8 us -> 21 us
    unnamed x14 -> x13, waiting for transfers between devices: 45.7 us -> 45.7 us
  transfers between devices with their start and end apart: 12 -> 13, of which waited for: 11 -> 12; matrix products, arithmetic and copies ran while one was open for 17% -> 16% of each run, Pallas kernels for 0% -> 0%
where the time goes in v1:
time: 768 us; the launch traced here: 761 us
  waiting for transfers between devices  461 us (60%)
  matrix products  110 us (14%)
  local copies, waits for them, and re-layouts  70.6 us (9%)
  other arithmetic  58.9 us (8%)
  blocking collectives  40.3 us (5%)
  between operations  14.5 us (2%)
    reduce_scatter x1, waiting for transfers between devices, per_device(): lax.psum_scatter(grad_up, 'dp', scatter_dimension=0, tiled=True)  72.2 us
    reduce_scatter x1, waiting for transfers between devices, per_device(): lax.psum_scatter(jnp.dot(piece, out_proj, preferred_element_type=jnp.floa...  59.9 us
    reduce_scatter x1, waiting for transfers between devices, per_device(): lax.psum_scatter(jnp.einsum('cte,cde->td', piece, in_proj, preferred_elem...  58.1 us
    reduce_scatter x1, waiting for transfers between devices, per_device(): lax.psum_scatter(jnp.einsum('tf,df->td', piece, up_proj, preferred_elemen...  47.2 us
    unnamed x13, waiting for transfers between devices  45.7 us
    psum x1, blocking collectives, per_device(): lax.psum((jnp.stack([gain_first, gain_second]), jnp.stack([bias_first, bi...  40.3 us
    reduce_scatter x1, waiting for transfers between devices, per_device(): lax.psum_scatter(jnp.dot(piece, down_proj, preferred_element_type=jnp.flo...  37.7 us
    ppermute x2, waiting for transfers between devices, grow_blocks(): lax.ppermute(tiles, axis, [(i, i ^ bit) for i in range(length)])  37.1 us
  transfers between devices with their start and end apart: 13, of which 12 were waited for; matrix products, arithmetic and copies ran while one was open for 16% of the time, Pallas kernels for 0%

profile of v1, /device:TPU:0, one launch (start us, length us, event | category | flops | bytes accessed | tf_op | source)
XLA Modules:
  0.0 761.0 jit_solution(6106946598555535306)
XLA Ops:
  21.6 35.0 %collective-permute-done.1 = bf16[2,512,768]{2,1,0:T(8,128)(2,1)} collective-permute-done((bf16[2,512,768]{2,1,0:T(8,128)(2,1)}, bf16[2,512,768]{2,1,0:T(8,128)(2,1)}, u32[]{:S(2)}, u32[]{:S(2)}) %collective-permute-start.1) | collective-permute-done | bytes 1572896 | tf_op jit(solution)/shard_map/ppermute | solution.py:21
  68.1 36.0 %while.58 = (s32[]{:T(128)}, bf16[2,2,512,192]{2,1,0,3:T(2,128)(2,1)}, f32[2,2,3,512]{3,2,1,0:T(4,128)}, bf16[2,2,512,192]{2,3,1,0:T(8,128)(2,1)}, bf16[2,1024,1...) while((s32[]{:T(128)}, ...), condition=%wide.region_7.8_spmd.clone, body=%wide.region_2.7_spmd.clone.sunk | while | flops 421625344 | bytes 24185224 | solution.py:93
  71.6 12.1 %while.61 = (s32[]{:T(128)}, bf16[2,512,192]{1,2,0:T(8,128)(2,1)S(1)}, f32[2,3,512]{2,1,0:T(4,128)}, s32[]{:T(128)}, s32[1024]{0:T(1024)S(1)}, /*index=5*/bf16[2...) while((s32[]{:T(128)}, ...), condition=%wide.region_6.6_spmd, body=%wide.region_3.5_spmd.sunk | while | flops 421625344 | bytes 21002412 | solution.py:91
  89.5 12.1 %while.61 = (s32[]{:T(128)}, bf16[2,512,192]{1,2,0:T(8,128)(2,1)S(1)}, f32[2,3,512]{2,1,0:T(4,128)}, s32[]{:T(128)}, s32[1024]{0:T(1024)S(1)}, /*index=5*/bf16[2...) while((s32[]{:T(128)}, ...), condition=%wide.region_6.6_spmd, body=%wide.region_3.5_spmd.sunk | while | flops 421625344 | bytes 21002412 | solution.py:91
  106.7 4.9 fusion.56
  111.7 59.9 %reduce-scatter.13.cloned.1.call-done = f32[512,768]{1,0:T(8,128)} async-done(((f32[2048,768]{1,0:T(8,128)}), f32[512,768]{1,0:T(8,128)}) %reduce-scatter.13.cloned.1.call-update) | async-done | bytes 1572880 | tf_op jit(solution)/shard_map/reduce_scatter | solution.py:96
  176.4 27.9 %all-gather.4.cloned.1.call-done = bf16[2048,768]{1,0:T(8,128)(2,1)} async-done(((bf16[512,768]{1,0:T(8,128)(2,1)}), bf16[2048,768]{1,0:T(8,128)(2,1)}) %all-gather.4.cloned.1.call-update) | async-done | bytes 3145744 | tf_op jit(solution)/shard_map/all_gather | solution.py:104
  204.3 7.5 fusion.57
  211.8 22.7 %all-gather.6.cloned.1.call-done = bf16[2048,768]{1,0:T(8,128)(2,1)} async-done(((bf16[512,768]{1,0:T(8,128)(2,1)}), bf16[2048,768]{1,0:T(8,128)(2,1)}) %all-gather.6.cloned.1.call-update) | async-done | bytes 3145744 | tf_op jit(solution)/shard_map/all_gather | solution.py:117
  234.5 19.3 %add_convert_fusion = (bf16[2048,768]{1,0:T(8,128)(2,1)S(1)}, f32[2048,768]{1,0:T(8,128)}) fusion(f32[2048,768]{1,0:T(8,128)} %fusion.57, bf16[2048,768]{1,0:T(8,128)(2,1)} %all-gather.6.cloned.1.call-done, bf16[768,768]{1,0:T(8,128)(2,1)S(1)} %copy-done), kind=kOutput, calls=%fused_computation.51 | convolution fusion | flops 2529165312 | bytes 20054016 | tf_op jit(solution)/shard_map/td,fd->tf/dot_general | solution.py:119
  255.5 4.5 fusion.58
  260.2 5.5 multiply_convert_fusion.1
  267.4 4.0 convolution_convert_fusion
  271.4 47.2 %reduce-scatter.17.cloned.1.call-done = f32[512,768]{1,0:T(8,128)} async-done(((f32[2048,768]{1,0:T(8,128)}), f32[512,768]{1,0:T(8,128)}) %reduce-scatter.17.cloned.1.call-update) | async-done | bytes 1572880 | tf_op jit(solution)/shard_map/reduce_scatter | solution.py:124
  321.2 37.7 %reduce-scatter.15.cloned.1.call-done = bf16[512,768]{1,0:T(8,128)(2,1)} async-done(((bf16[2048,768]{1,0:T(8,128)(2,1)}), bf16[512,768]{1,0:T(8,128)(2,1)}) %reduce-scatter.15.cloned.1.call-update) | async-done | bytes 786448 | tf_op jit(solution)/shard_map/reduce_scatter | solution.py:110
  359.0 3.1 fusion.50
  364.6 28.6 %all-gather.8.cloned.1.call-done = bf16[2048,768]{1,0:T(8,128)(2,1)} async-done(((bf16[512,768]{1,0:T(8,128)(2,1)}), bf16[2048,768]{1,0:T(8,128)(2,1)}) %all-gather.8.cloned.1.call-update) | async-done | bytes 3145744 | tf_op jit(solution)/shard_map/all_gather | solution.py:132
  396.9 4.1 convolution_bitcast_fusion.2
  401.1 63.1 %while.60 = (s32[]{:T(128)}, bf16[2,1024,192]{2,1,0:T(8,128)(2,1)}, bf16[2,1024,192]{1,2,0:T(8,128)(2,1)}, bf16[2,1024,192]{1,2,0:T(8,128)(2,1)}, bf16[2,2,512,1...) while((s32[]{:T(128)}, bf16[2,1024,192]{2,1,0:T(8,128)(2,1)}, ...), condition=%wide.region_19.20_spmd.clone, body=%wide.region_15.19_spmd.clone.sunk | while | flops 1031798272 | bytes 92420848 | solution.py:190
  406.6 21.5 %while.62 = (s32[]{:T(128)}, f32[1024,3,64]{0,2,1:T(8,128)S(1)}, f32[1024,3,64]{0,2,1:T(8,128)}, bf16[2,512,192]{1,2,0:T(8,128)(2,1)}, bf16[2,512,192]{1,2,0:T(8...) while((s32[]{:T(128)}, f32[1024,3,64]{0,2,1:T(8,128)S(1)}, ...), condition=%wide.region_18.18_spmd.clone, body=%wide.region_16.17_spmd.clone.sunk | while | flops 1031405056 | bytes 63162644 | solution.py:180
  438.0 21.5 %while.62 = (s32[]{:T(128)}, f32[1024,3,64]{0,2,1:T(8,128)S(1)}, f32[1024,3,64]{0,2,1:T(8,128)}, bf16[2,512,192]{1,2,0:T(8,128)(2,1)}, bf16[2,512,192]{1,2,0:T(8...) while((s32[]{:T(128)}, f32[1024,3,64]{0,2,1:T(8,128)S(1)}, ...), condition=%wide.region_18.18_spmd.clone, body=%wide.region_16.17_spmd.clone.sunk | while | flops 1031405056 | bytes 63162644 | solution.py:180
  469.9 4.1 convolution_bitcast_fusion.1
  476.8 4.8 reshape.223
  481.7 4.6 convolution_bitcast_fusion
  486.4 7.0 fusion.60
  493.7 7.0 fusion.59
  503.6 44.8 %reduce-scatter.25.cloned.1.call-done = f32[96,576]{1,0:T(8,128)} async-done(((f32[768,576]{1,0:T(8,128)}), f32[96,576]{1,0:T(8,128)}) %reduce-scatter.25.cloned.1.call-update) | async-done | bytes 221200
  550.3 58.1 %reduce-scatter.19.cloned.1.call-done = f32[512,768]{1,0:T(8,128)} async-done(((f32[2048,768]{1,0:T(8,128)}), f32[512,768]{1,0:T(8,128)}) %reduce-scatter.19.cloned.1.call-update) | async-done | bytes 1572880 | tf_op jit(solution)/shard_map/reduce_scatter | solution.py:202
  614.4 40.3 %all-reduce = (f32[2,768]{1,0:T(2,128)}, f32[2,768]{1,0:T(2,128)}) all-reduce(f32[2,768]{1,0:T(2,128)} %pad_maximum_fusion.5, f32[2,768]{1,0:T(2,128)} %pad_maximum_fusion.6), channel_id=1, replica_groups=mesh['dp'=8,'tensor'=4] {'dp','tensor'}, use_global_device_ids=true, to_apply=%region_29.30 | all-reduce | flops 3072 | bytes 24576 | tf_op jit(solution)/shard_map/psum | solution.py:210
  655.4 3.2 add_convert_fusion.1
  658.6 23.4 %reduce-scatter.23.cloned.1.call-done = f32[768,96]{0,1:T(8,128)} async-done(((f32[768,768]{0,1:T(8,128)}), f32[768,96]{0,1:T(8,128)}) %reduce-scatter.23.cloned.1.call-update) | async-done | bytes 294928 | tf_op jit(solution)/shard_map/reduce_scatter | solution.py:218
  682.0 72.2 %reduce-scatter.21.cloned.1.call-done = f32[96,768]{1,0:T(8,128)} async-done(((f32[768,768]{1,0:T(8,128)}), f32[96,768]{1,0:T(8,128)}) %reduce-scatter.21.cloned.1.call-update) | async-done | bytes 294928 | tf_op jit(solution)/shard_map/reduce_scatter | solution.py:217
  (343 shorter events, 163.2 us)
Async XLA Ops:
  7.2 227.4 %copy-start = (bf16[768,768]{1,0:T(8,128)(2,1)S(1)}, bf16[768,768]{1,0:T(8,128)(2,1)}, u32[]{:S(2)}) copy-start(bf16[768,768]{1,0:T(8,128)(2,1)} %param.22) | copy-start | bytes 3538948
  7.2 8.5 %copy-start.2 = (bf16[512,768]{1,0:T(8,128)(2,1)S(1)}, bf16[512,768]{1,0:T(8,128)(2,1)}, u32[]{:S(2)}) copy-start(bf16[512,768]{1,0:T(8,128)(2,1)} %param.17) | copy-start | bytes 2359300
  7.2 164.4 %reduce-scatter.13.cloned.1.call-start = ((), (), s32[]{:S(2)}) async-start(), calls=%async_computation.8 | async-start | bytes 7864320 | tf_op jit(solution)/shard_map/reduce_scatter | solution.py:96
  8.7 10.0 %copy-start.32 = (f32[512]{0:T(512)}, f32[512]{0:T(512)S(1)}, u32[]{:S(2)}) copy-start(f32[512]{0:T(512)S(1)} %broadcast_multiply_fusion.1) | copy-start | bytes 6148
  10.2 8.5 %copy-start.35 = (f32[512]{0:T(512)}, f32[512]{0:T(512)S(1)}, u32[]{:S(2)}) copy-start(f32[512]{0:T(512)S(1)} %fusion.44) | copy-start | bytes 6148
  13.1 2.6 collective-permute-start
  18.7 37.9 %collective-permute-start.1 = (bf16[2,512,768]{2,1,0:T(8,128)(2,1)}, bf16[2,512,768]{2,1,0:T(8,128)(2,1)}, u32[]{:S(2)}, u32[]{:S(2)}) collective-permute-start(bf16[2,512,768]{2,1,0:T(8,128)(2,1)} %pad_maximum_fusion.2), channel_id=1, source_target_pairs={{0,2},{1,3},{2,0},{3,1},{4,6},{5,7},{6,4},{7,5},{8,10},{9,11},{10,... | collective-permute-start | bytes 4718600 | tf_op jit(solution)/shard_map/ppermute | solution.py:21
  111.6 60.0 %copy-start.3 = (bf16[512,768]{1,0:T(8,128)(2,1)S(1)}, bf16[512,768]{1,0:T(8,128)(2,1)}, u32[]{:S(2)}) copy-start(bf16[512,768]{1,0:T(8,128)(2,1)} %param.17) | copy-start | bytes 2359300
  111.6 62.8 %copy-start.34 = (f32[768]{0:T(1024)S(1)}, f32[768]{0:T(1024)}, u32[]{:S(2)}) copy-start(f32[768]{0:T(1024)} %get-tuple-element.501) | copy-start | bytes 9220
  111.6 62.8 %copy-start.40 = (f32[768]{0:T(1024)S(1)}, f32[768]{0:T(1024)}, u32[]{:S(2)}) copy-start(f32[768]{0:T(1024)} %get-tuple-element.400) | copy-start | bytes 9220
  111.6 92.7 %all-gather.4.cloned.1.call-start = ((), (), s32[]{:S(2)}) async-start(), calls=%async_computation.9 | async-start | bytes 3932160 | tf_op jit(solution)/shard_map/all_gather | solution.py:104
  175.6 58.9 %all-gather.6.cloned.1.call-start = ((), (), s32[]{:S(2)}) async-start(), calls=%async_computation.11 | async-start | bytes 3932160 | tf_op jit(solution)/shard_map/all_gather | solution.py:117
  176.3 142.3 %reduce-scatter.17.cloned.1.call-start = ((), (), s32[]{:S(2)}) async-start(), calls=%async_computation.12 | async-start | bytes 7864320 | tf_op jit(solution)/shard_map/reduce_scatter | solution.py:124
  211.8 43.8 %copy-start.43 = (bf16[768,768]{1,0:T(8,128)(2,1)S(1)}, bf16[768,768]{1,0:T(8,128)(2,1)}, u32[]{:S(2)}) copy-start(bf16[768,768]{1,0:T(8,128)(2,1)} %param.21) | copy-start | bytes 3538948
  260.1 98.9 %reduce-scatter.15.cloned.1.call-start = ((), (), s32[]{:S(2)}) async-start(), calls=%async_computation.10 | async-start | bytes 3932160 | tf_op jit(solution)/shard_map/reduce_scatter | solution.py:110
  271.3 47.3 %copy-start.6 = (f32[512,768]{1,0:T(8,128)S(1)}, f32[512,768]{1,0:T(8,128)}, u32[]{:S(2)}) copy-start(f32[512,768]{1,0:T(8,128)} %copy-done.5) | copy-start | bytes 4718596
  271.4 121.8 %all-gather.8.cloned.1.call-start = ((), (), s32[]{:S(2)}) async-start(), calls=%async_computation.13 | async-start | bytes 3932160 | tf_op jit(solution)/shard_map/all_gather | solution.py:132
  321.2 42.1 %copy-start.15 = (bf16[512,768]{1,0:T(8,128)(2,1)S(1)}, bf16[512,768]{1,0:T(8,128)(2,1)}, u32[]{:S(2)}) copy-start(bf16[512,768]{1,0:T(8,128)(2,1)} %param.25) | copy-start | bytes 2359300
  362.1 31.1 %copy-start.29 = (bf16[192,768]{1,0:T(8,128)(2,1)S(1)}, bf16[192,768]{1,0:T(8,128)(2,1)}, u32[]{:S(2)}) copy-start(bf16[192,768]{1,0:T(8,128)(2,1)} %param.20) | copy-start | bytes 884740
  362.1 34.1 %copy-start.39 = (f32[512]{0:T(512)}, f32[512]{0:T(512)S(1)}, u32[]{:S(2)}) copy-start(f32[512]{0:T(512)S(1)} %negate_multiply_fusion.2) | copy-start | bytes 6148
  364.5 137.5 %reduce-scatter.27.cloned.1.call-start = ((), (), s32[]{:S(2)}) async-start(), calls=%async_computation.18 | async-start | bytes 884736
  364.6 32.3 %copy-start.17 = (bf16[2048,192]{0,1:T(8,128)(2,1)S(1)}, bf16[2048,192]{0,1:T(8,128)(2,1)}, u32[]{:S(2)}) copy-start(bf16[2048,192]{0,1:T(8,128)(2,1)} %copy-done.16) | copy-start | bytes 2359300
  401.0 147.4 %reduce-scatter.25.cloned.1.call-start = ((), (), s32[]{:S(2)}) async-start(), calls=%async_computation.17 | async-start | bytes 2211840
  481.6 126.8 %reduce-scatter.19.cloned.1.call-start = ((), (), s32[]{:S(2)}) async-start(), calls=%async_computation.14 | async-start | bytes 7864320 | tf_op jit(solution)/shard_map/reduce_scatter | solution.py:202
  486.3 195.7 %reduce-scatter.23.cloned.1.call-start = ((), (), s32[]{:S(2)}) async-start(), calls=%async_computation.16 | async-start | bytes 2654208 | tf_op jit(solution)/shard_map/reduce_scatter | solution.py:218
  493.5 260.8 %reduce-scatter.21.cloned.1.call-start = ((), (), s32[]{:S(2)}) async-start(), calls=%async_computation.15 | async-start | bytes 2654208 | tf_op jit(solution)/shard_map/reduce_scatter | solution.py:217
  500.8 107.7 %copy-start.4 = (bf16[512,768]{1,0:T(8,128)(2,1)S(1)}, bf16[512,768]{1,0:T(8,128)(2,1)}, u32[]{:S(2)}) copy-start(bf16[512,768]{1,0:T(8,128)(2,1)} %param.17) | copy-start | bytes 2359300
  500.8 107.7 %copy-start.31 = (f32[768]{0:T(1024)S(1)}, f32[768]{0:T(1024)}, u32[]{:S(2)}) copy-start(f32[768]{0:T(1024)} %copy-done.30) | copy-start | bytes 9220
  500.8 107.7 %copy-start.33 = (f32[512]{0:T(512)S(1)}, f32[512]{0:T(512)}, u32[]{:S(2)}) copy-start(f32[512]{0:T(512)} %copy-done.32) | copy-start | bytes 6148
  500.8 109.7 %copy-start.38 = (f32[512]{0:T(512)S(1)}, f32[512]{0:T(512)}, u32[]{:S(2)}) copy-start(f32[512]{0:T(512)} %copy-done.37) | copy-start | bytes 6148
  500.8 109.7 %copy-start.36 = (f32[512]{0:T(512)S(1)}, f32[512]{0:T(512)}, u32[]{:S(2)}) copy-start(f32[512]{0:T(512)} %copy-done.35) | copy-start | bytes 6148
  610.5 143.8 %copy-start.1 = (bf16[768,768]{1,0:T(8,128)(2,1)S(1)}, bf16[768,768]{1,0:T(8,128)(2,1)}, u32[]{:S(2)}) copy-start(bf16[768,768]{1,0:T(8,128)(2,1)} %param.22) | copy-start | bytes 3538948
  (52 other events, 121.0 us)
Sparse Core Ops, SparseCore 0:
  111.7 59.8 reduce-scatter.12
  175.7 28.5 all-gather.3
  206.0 28.5 all-gather.5
  260.2 58.3 reduce-scatter.16
  321.0 37.9 reduce-scatter.14
  364.6 28.5 all-gather.7
  401.1 62.3 reduce-scatter.26
  481.8 66.6 reduce-scatter.24
  551.2 57.2 reduce-scatter.18
  612.4 69.5 reduce-scatter.22
  686.1 68.1 reduce-scatter.20
